TPU v7x, 32 devices: a whole 2x2x4 slice. The times are simulated.
32 devices in a mesh: req: 8 (over y, x, core), mdl: 4 (over z).
Axes of the slice: x: 2, y: 2, z: 4, core: 2. Of those that a mesh axis runs over, the one named last changes fastest.
Arguments:
- tokens: bfloat16 [256, 4, 2048], P('req', None, 'mdl'), may hold values from -6 to 6
- counts: int32 [256], P('req'), may hold values from 1 to 4
- new_owner: int32 [256], replicated, may hold values from 0 to 255, as said below
- wkv_state: float32 [256, 32, 4096], P('req', 'mdl'), may hold values from -12 to 12
- att_shift: bfloat16 [256, 2048], P('req', 'mdl'), may hold values from -6 to 6
- ffn_shift: bfloat16 [256, 2048], P('req', 'mdl'), may hold values from -6 to 6
- norm_params: float32 [4, 2048], replicated, may hold values from 0.25 to 1.75
- mix_coeffs: float32 [7, 2048], replicated, may hold values from 0 to 1
- head_params: float32 [7, 2048], P(None, 'mdl'), may hold values from -6 to 2
- recept_weight: bfloat16 [2048, 2048], P(None, 'mdl'), may hold values from -0.125 to 0.125
- key_weight: bfloat16 [2048, 2048], P(None, 'mdl'), may hold values from -0.125 to 0.125
- value_weight: bfloat16 [2048, 2048], P(None, 'mdl'), may hold values from -0.125 to 0.125
- output_weight: bfloat16 [2048, 2048], P('mdl'), may hold values from -0.125 to 0.125
- decay_down: bfloat16 [2048, 96], P('mdl'), may hold values from -0.125 to 0.125
- decay_up: bfloat16 [96, 2048], P(None, 'mdl'), may hold values from -0.625 to 0.625
- alpha_down: bfloat16 [2048, 96], P('mdl'), may hold values from -0.125 to 0.125
- alpha_up: bfloat16 [96, 2048], P(None, 'mdl'), may hold values from -0.625 to 0.625
- gate_down: bfloat16 [2048, 256], P('mdl'), may hold values from -0.125 to 0.125
- gate_up: bfloat16 [256, 2048], P(None, 'mdl'), may hold values from -0.375 to 0.375
- ffn_key_weight: bfloat16 [2048, 4096], P(None, 'mdl'), may hold values from -0.125 to 0.125
- ffn_value_weight: bfloat16 [4096, 2048], P('mdl'), may hold values from -0.09375 to 0.09375
Outputs:
- block_output: bfloat16 [256, 4, 2048], P('req', None, 'mdl')
- new_state: float32 [256, 32, 4096], P('req', 'mdl')
- new_att_shift: bfloat16 [256, 2048], P('req', 'mdl')
- new_ffn_shift: bfloat16 [256, 2048], P('req', 'mdl')
Inputs may be any that keep to these rules, and one draw needn't show every extreme that they name: new_owner is a permutation: the states of request i move to position new_owner[i]. Of the 32 requests of each aligned block of positions, exactly 4 move into each aligned block.
All inputs are finite; a program needn't handle non-finite values.
Results may differ from a plain program's by a relative error of at most 0.0095.
Values may be sent and summed in bfloat16 or wider, within the bound.
No kernel may reach another device: no remote copies, remote signals or barrier semaphores. Data moves between devices by JAX's collectives and lax.ppermute only.
A program may use at most 256 MiB of HBM per device.

v0:
```python
import jax
import jax.numpy as jnp
from jax import lax
from jax.sharding import PartitionSpec as P


def layer_norm(stream, gain_row, offset):
    center = stream - jnp.mean(stream, axis=-1, keepdims=True)
    spread = jnp.mean(center * center, axis=-1, keepdims=True)
    return center / jnp.sqrt(spread + 1e-05) * gain_row + offset


def project(inputs, weight):
    return jnp.dot(inputs, weight, preferred_element_type=jnp.float32)


def split_heads(source, head_size):
    sequence_batch_count, decode_loop_steps_count, feature_count = source.shape
    return source.reshape(
        sequence_batch_count, decode_loop_steps_count, feature_count // head_size, head_size
    )


def advance(wkv_square, decay_now, key_now, value_now, unit_now, alpha_now, recept_now, is_valid):
    removal = -jnp.sum(wkv_square * unit_now[:, :, None, :], axis=-1)
    updated = (
        wkv_square * decay_now[:, :, None, :]
        + removal[..., None] * (unit_now * alpha_now)[:, :, None, :]
        + value_now[..., None] * key_now[:, :, None, :]
    )
    memory_matrix_product = jnp.sum(updated * recept_now[:, :, None, :], axis=-1)
    return (jnp.where(is_valid[:, None, None, None], updated, wkv_square), memory_matrix_product)


def prepare_keys(key_proj, in_context, learned_weights, head_size):
    scaled = split_heads(key_proj * learned_weights[2], head_size)
    key_unit = scaled / jnp.sqrt(jnp.sum(scaled * scaled, axis=-1, keepdims=True) + 1e-06)
    lookup_adjust_factor = key_proj * (1.0 + (in_context - 1.0) * learned_weights[3])
    return (key_unit.reshape(key_proj.shape), lookup_adjust_factor)


def run_heads(
    wkv_flat,
    decay_rate,
    lookup_adjust_factor,
    values,
    key_unit,
    in_context,
    acceptance_matrix_lines,
    live_mask,
    head_size,
):
    sequence_batch_count, decode_loop_steps_count, feature_count = acceptance_matrix_lines.shape
    head_count = feature_count // head_size
    decay_heads = split_heads(decay_rate, head_size)
    keymod_heads = split_heads(lookup_adjust_factor, head_size)
    payload_each_group = split_heads(values, head_size)
    unit_heads = split_heads(key_unit, head_size)
    alpha_heads = split_heads(in_context, head_size)
    recept_heads = split_heads(acceptance_matrix_lines, head_size)
    wkv_square = wkv_flat.reshape(sequence_batch_count, head_count, head_size, head_size)
    readouts = []
    for position in range(decode_loop_steps_count):
        wkv_square, memory_matrix_product = advance(
            wkv_square,
            decay_heads[:, position],
            keymod_heads[:, position],
            payload_each_group[:, position],
            unit_heads[:, position],
            alpha_heads[:, position],
            recept_heads[:, position],
            live_mask[:, position] > 0.5,
        )
        readouts.append(memory_matrix_product)
    stacked = jnp.stack(readouts, axis=1).reshape(
        sequence_batch_count, decode_loop_steps_count, feature_count
    )
    return (stacked, wkv_square.reshape(sequence_batch_count, head_count, head_size * head_size))


def finish_heads(
    memory_matrix_product,
    acceptance_matrix_lines,
    lookup_adjust_factor,
    values,
    sigmoid_scaling_entries,
    learned_weights,
    head_size,
):
    stacked = split_heads(memory_matrix_product, head_size)
    center = stacked - jnp.mean(stacked, axis=-1, keepdims=True)
    spread = jnp.mean(center * center, axis=-1, keepdims=True)
    layernormed_activations = (center / jnp.sqrt(spread + 0.00064)).reshape(
        memory_matrix_product.shape
    ) * learned_weights[5] + learned_weights[6]
    extra_term_share = jnp.sum(
        split_heads(acceptance_matrix_lines * lookup_adjust_factor * learned_weights[4], head_size),
        axis=-1,
        keepdims=True,
    ) * split_heads(values, head_size)
    return (
        (layernormed_activations + extra_term_share.reshape(memory_matrix_product.shape))
        * sigmoid_scaling_entries
    ).astype(jnp.bfloat16)


def per_device(
    tokens,
    counts,
    new_owner,
    wkv_state,
    att_shift,
    ffn_shift,
    norm_params,
    mix_coeffs,
    head_params,
    recept_weight,
    key_weight,
    value_weight,
    output_weight,
    decay_down,
    decay_up,
    alpha_down,
    alpha_up,
    gate_down,
    gate_up,
    ffn_key_weight,
    ffn_value_weight,
):
    groups = lax.axis_size("req")
    sequence_batch_count, decode_loop_steps_count, local_width = tokens.shape
    per_pair = sequence_batch_count // groups
    req_rank = lax.axis_index("req")
    column_start = lax.axis_index("mdl") * local_width
    head_size = local_width // wkv_state.shape[1]
    row_count = sequence_batch_count * decode_loop_steps_count
    shape_three = (sequence_batch_count, decode_loop_steps_count, local_width)
    slot_ids = jnp.arange(decode_loop_steps_count, dtype=jnp.int32)
    live_mask = (slot_ids[None, :] < counts[:, None]).astype(jnp.float32)
    own_block = lax.dynamic_slice_in_dim(
        new_owner, req_rank * sequence_batch_count, sequence_batch_count
    )
    sending = jnp.argsort(own_block)
    sorted_rows = jnp.sort(new_owner.reshape(groups, sequence_batch_count), axis=1)
    arriving = (
        lax.dynamic_slice_in_dim(sorted_rows, req_rank * per_pair, per_pair, 1)
        - req_rank * sequence_batch_count
    )
    placing = jnp.argsort(arriving.reshape(-1))
    sent_state = wkv_state[sending].reshape((groups, per_pair) + wkv_state.shape[1:])
    sent_att = att_shift[sending].astype(jnp.float32).reshape(groups, per_pair, local_width)
    sent_ffn = ffn_shift[sending].astype(jnp.float32).reshape(groups, per_pair, local_width)
    got_state, got_att, got_ffn = (
        lax.all_to_all(sent_state, "req", split_axis=0, concat_axis=0, tiled=True),
        lax.all_to_all(sent_att, "req", split_axis=0, concat_axis=0, tiled=True),
        lax.all_to_all(sent_ffn, "req", split_axis=0, concat_axis=0, tiled=True),
    )
    moved_state = got_state.reshape((sequence_batch_count,) + wkv_state.shape[1:])[placing]
    moved_att = got_att.reshape(sequence_batch_count, local_width)[placing].astype(jnp.bfloat16)
    moved_ffn = got_ffn.reshape(sequence_batch_count, local_width)[placing].astype(jnp.bfloat16)
    full_tokens = lax.all_gather(tokens, "mdl", axis=2, tiled=True)
    full_stream = full_tokens.astype(jnp.float32)
    entire_channel_count = full_tokens.shape[2]
    prev_att, prev_ffn = (
        lax.all_gather(moved_att, "mdl", axis=1, tiled=True),
        lax.all_gather(moved_ffn, "mdl", axis=1, tiled=True),
    )
    normed_one = layer_norm(full_stream, norm_params[0], norm_params[1])
    before_one = jnp.concatenate(
        [prev_att.astype(jnp.float32)[:, None], normed_one[:, :-1]], axis=1
    )
    delta_one = before_one - normed_one
    normed_local = lax.dynamic_slice_in_dim(normed_one, column_start, local_width, 2)

    def mixed_input(mix_index):
        return (
            (normed_one + delta_one * mix_coeffs[mix_index])
            .astype(jnp.bfloat16)
            .reshape(row_count, entire_channel_count)
        )

    decay_full, alpha_full, gate_full = (
        lax.all_gather(decay_down, "mdl", axis=0, tiled=True),
        lax.all_gather(alpha_down, "mdl", axis=0, tiled=True),
        lax.all_gather(gate_down, "mdl", axis=0, tiled=True),
    )
    decay_sum = project(mixed_input(1), decay_full)
    alpha_sum = project(mixed_input(4), alpha_full)
    gate_sum = project(mixed_input(5), gate_full)
    decay_low = jnp.tanh(decay_sum).astype(jnp.bfloat16)
    alpha_low = alpha_sum.astype(jnp.bfloat16)
    gate_low = jax.nn.sigmoid(gate_sum).astype(jnp.bfloat16)
    decay_rate = jnp.exp(
        -0.606531 * jax.nn.sigmoid(head_params[0] + project(decay_low, decay_up))
    ).reshape(shape_three)
    in_context = jax.nn.sigmoid(head_params[1] + project(alpha_low, alpha_up)).reshape(shape_three)
    sigmoid_scaling_entries = project(gate_low, gate_up).reshape(shape_three)
    acceptance_matrix_lines = project(mixed_input(0), recept_weight).reshape(shape_three)
    key_proj = project(mixed_input(2), key_weight).reshape(shape_three)
    values = project(mixed_input(3), value_weight).reshape(shape_three)
    key_unit, lookup_adjust_factor = prepare_keys(key_proj, in_context, head_params, head_size)
    memory_matrix_product, new_state = run_heads(
        moved_state,
        decay_rate,
        lookup_adjust_factor,
        values,
        key_unit,
        in_context,
        acceptance_matrix_lines,
        live_mask,
        head_size,
    )
    attention_group_result = finish_heads(
        memory_matrix_product,
        acceptance_matrix_lines,
        lookup_adjust_factor,
        values,
        sigmoid_scaling_entries,
        head_params,
        head_size,
    )
    attended_term = project(attention_group_result.reshape(row_count, local_width), output_weight)
    attended = lax.psum_scatter(attended_term, "mdl", scatter_dimension=1, tiled=True).reshape(
        shape_three
    )
    midstream = (tokens.astype(jnp.float32) + attended).astype(jnp.bfloat16)
    full_mid = lax.all_gather(midstream, "mdl", axis=2, tiled=True)
    normed_two = layer_norm(full_mid.astype(jnp.float32), norm_params[2], norm_params[3])
    before_two = jnp.concatenate(
        [prev_ffn.astype(jnp.float32)[:, None], normed_two[:, :-1]], axis=1
    )
    ffn_in = (
        (normed_two + (before_two - normed_two) * mix_coeffs[6])
        .astype(jnp.bfloat16)
        .reshape(row_count, entire_channel_count)
    )
    hidden = jnp.square(jax.nn.relu(project(ffn_in, ffn_key_weight))).astype(jnp.bfloat16)
    ffn_out = (
        lax.psum_scatter(
            project(hidden, ffn_value_weight).astype(jnp.bfloat16),
            "mdl",
            scatter_dimension=1,
            tiled=True,
        )
        .astype(jnp.float32)
        .reshape(shape_three)
    )
    block_output = jnp.where(
        live_mask[..., None] > 0.5, midstream.astype(jnp.float32) + ffn_out, 0.0
    ).astype(jnp.bfloat16)
    chosen = (slot_ids[None, :] == (counts - 1)[:, None]).astype(jnp.float32)
    normed_two_local = lax.dynamic_slice_in_dim(normed_two, column_start, local_width, 2)
    new_att_shift = jnp.sum(normed_local * chosen[..., None], axis=1).astype(jnp.bfloat16)
    new_ffn_shift = jnp.sum(normed_two_local * chosen[..., None], axis=1).astype(jnp.bfloat16)
    return (block_output, new_state, new_att_shift, new_ffn_shift)


def solution(mesh):
    return jax.shard_map(
        per_device,
        mesh=mesh,
        in_specs=(
            P("req", None, "mdl"),
            P("req"),
            P(),
            P("req", "mdl", None),
            P("req", "mdl"),
            P("req", "mdl"),
            P(),
            P(),
            P(None, "mdl"),
            P(None, "mdl"),
            P(None, "mdl"),
            P(None, "mdl"),
            P("mdl", None),
            P("mdl", None),
            P(None, "mdl"),
            P("mdl", None),
            P(None, "mdl"),
            P("mdl", None),
            P(None, "mdl"),
            P(None, "mdl"),
            P("mdl", None),
        ),
        out_specs=(P("req", None, "mdl"), P("req", "mdl", None), P("req", "mdl"), P("req", "mdl")),
        check_vma=False,
    )
```

profile of v0, /device:TPU:0, one launch (start us, length us, event | category | flops | bytes accessed | tf_op | source)
XLA Modules:
  0.0 439.1 jit_solution(6680961267923316029)
XLA Ops:
  12.3 5.2 %all-to-all-start.1 = ((bf16[8,4,512]{2,1,0:T(4,128)(2,1)}), bf16[8,4,512]{2,1,0:T(4,128)(2,1)S(1)}, u32[]{:S(2)}, u32[]{:S(2)}) async-start(bf16[8,4,512]{2,1,0:T(4,128)(2,1)} %reshape.354), calls=%async_computation.1 | async-start | bytes 65536 | tf_op jit(solution)/shard_map/all_to_all | solution.py:155
  27.7 20.2 %all_gather.23 = bf16[2048,96]{0,1:T(8,128)(2,1)} all-gather(bf16[512,96]{0,1:T(8,128)(2,1)} %param.34), channel_id=1, replica_groups=mesh['req'=8,'mdl'=4] {'mdl'}, dimensions={0}, use_global_device_ids=true | all-gather | bytes 491520 | tf_op jit(solution)/shard_map/all_gather | solution.py:183
  47.9 15.2 %all_gather.24 = bf16[2048,96]{0,1:T(8,128)(2,1)S(1)} all-gather(bf16[512,96]{0,1:T(8,128)(2,1)} %param.36), channel_id=1, replica_groups=mesh['req'=8,'mdl'=4] {'mdl'}, dimensions={0}, use_global_device_ids=true | all-gather | bytes 491520 | tf_op jit(solution)/shard_map/all_gather | solution.py:184
  63.2 14.9 %all_gather.21 = bf16[32,4,2048]{2,1,0:T(4,128)(2,1)S(1)} all-gather(bf16[32,4,512]{2,1,0:T(4,128)(2,1)} %param.21), channel_id=1, replica_groups=mesh['req'=8,'mdl'=4] {'mdl'}, dimensions={2}, use_global_device_ids=true | all-gather | bytes 655360 | tf_op jit(solution)/shard_map/all_gather | solution.py:161
  80.4 3.9 copy.89
  84.3 5.0 %gather_fusion = f32[32,8,4096]{2,1,0:T(8,128)} fusion(f32[32,8,4096]{2,1,0:T(8,128)} %param.24, s32[1024]{0:T(1024)S(1)} %pad_clamp_fusion.1), kind=kCustom, calls=%fused_computation | custom fusion | bytes 8388736 | tf_op jit(solution)/shard_map/gather | solution.py:150
  89.4 4.8 %all-to-all-start = ((f32[8,4,8,4096]{3,2,1,0:T(8,128)}), f32[8,4,8,4096]{3,2,1,0:T(8,128)}, u32[]{:S(2)}, u32[]{:S(2)}) async-start(f32[8,4,8,4096]{3,2,1,0:T(8,128)} %bitcast.175), calls=%async_computation | async-start | bytes 8388608 | tf_op jit(solution)/shard_map/all_to_all | solution.py:154
  94.9 13.7 %all_gather.22 = bf16[32,2048]{1,0:T(8,128)(2,1)S(1)} all-gather(bf16[32,512]{1,0:T(8,128)(2,1)S(1)} %gather_fusion.3), channel_id=1, replica_groups=mesh['req'=8,'mdl'=4] {'mdl'}, dimensions={1}, use_global_device_ids=true | all-gather | bytes 163840 | tf_op jit(solution)/shard_map/all_gather | solution.py:165
  108.8 3.5 add_convert_fusion.1
  112.3 2.0 reshape.344
  114.3 2.2 fusion.61
  118.2 1.9 reshape.348
  120.2 4.4 %add_convert_fusion.5 = (bf16[32,4,2048]{2,1,0:T(4,128)(2,1)}, bf16[32,4,2048]{2,1,0:T(4,128)(2,1)}, bf16[32,4,2048]{2,1,0:T(4,128)(2,1)}, bf16[32,4,2048,1]{2,1,0,3:T(4,128)(2,1)}) fusion(f32[2048]{0:T(1024)} %bitcast.202, f32[32,3,2048]{2,1,0:T(4,128)} %bitcast.177, f32[32,1,2048]{2,1,0:T(1,128)S(1)} %copy.86, f32[2048]{0:T(1024)} %bitcast.190, ...), kind=kLoop, calls=%fused_computation.82 | loop fusion | flops 4980736 | bytes 3720192 | tf_op jit(solution)/shard_map/convert_element_type | solution.py:178
  129.6 2.2 broadcast_add_fusion
  131.8 2.5 fusion.39
  137.0 3.8 broadcast_multiply_fusion.8
  154.7 2.3 fusion.23
  157.1 5.1 %gather_fusion.1 = f32[32,8,4096]{2,1,0:T(8,128)} fusion(f32[32,8,4096]{2,1,0:T(8,128)} %bitcast.1, s32[1024]{0:T(1024)} %copy-done.21), kind=kCustom, calls=%fused_computation.1 | custom fusion | bytes 8388736 | tf_op jit(solution)/shard_map/gather | solution.py:158
  162.2 8.3 %reshape.338 = f32[32,8,64,64]{3,2,1,0:T(8,128)} reshape(f32[32,8,4096]{2,1,0:T(8,128)} %gather_fusion.1) | data formatting | bytes 8388608 | tf_op jit(solution)/shard_map/reshape | solution.py:61
  170.5 5.8 %multiply_reduce_fusion.7 = f32[32,8,64]{2,1,0:T(8,128)S(1)} fusion(f32[32,8,64,64]{3,2,1,0:T(8,128)} %reshape.338, f32[32,8,64]{2,1,0:T(8,128)S(1)} %get-tuple-element.90), kind=kLoop, calls=%fused_computation.16 | loop fusion | flops 2080768 | bytes 4325376 | tf_op jit(solution)/shard_map/reduce_sum | solution.py:25
  176.4 11.0 %multiply_reduce_fusion.6 = (f32[32,8,64]{2,1,0:T(8,128)S(1)}, f32[32,8,64]{2,1,0:T(8,128)S(1)}) fusion(f32[32,8,64]{2,1,0:T(8,128)S(1)} %copy-done.8, f32[32,8,64,64]{3,2,1,0:T(8,128)S(1)} %copy-done.2, f32[32,8,64]{2,1,0:T(8,128)S(1)} %get-tuple-element.51, f32[32,8,64]{2,1,0:T(8,128)S(1)} %get-tuple-element.30, f32[32,8,64]{2,1,0:T(8,128)S(1)} %neg.38, ...), kind=kLoop, calls=%fused_computation.14 | loop fusion | flops 10452992 | bytes 4784160 | tf_op jit(solution)/shard_map/reduce_sum | solution.py:31
  188.8 18.7 %multiply_reduce_fusion.3 = (f32[32,8,64]{2,1,0:T(8,128)S(1)}, f32[32,8,64,64]{3,2,1,0:T(8,128)}, f32[32,8,64]{2,1,0:T(8,128)S(1)}, f32[32,8,64,64]{3,2,1,0:T(8,...) fusion(f32[32,8,64]{2,1,0:T(8,128)} %get-tuple-element.92, ...), kind=kLoop, calls=%fused_computation.10 | loop fusion | flops 16744448 | bytes 26083392 | tf_op jit(solution)/shard_map/reduce_sum | solution.py:25
  208.3 12.5 %multiply_reduce_fusion.2 = (f32[32,8,64]{2,1,0:T(8,128)S(1)}, f32[32,8,64]{2,1,0:T(8,128)S(1)}, f32[32,8,64,64]{3,2,1,0:T(8,128)}, f32[32,8,64,64]{3,2,1,0:T(8,128)}) fusion(f32[32,8,64]{2,1,0:T(8,128)} %get-tuple-element.34, f32[32,8,64,64]{3,2,1,0:T(8,128)} %get-tuple-element.18, f32[32,8,64]{2,1,0:T(8,128)S(1)} %get-tuple-element.48, ...), kind=kLoop, calls=%fused_computation.8 | loop fusion | flops 10452992 | bytes 13172768 | tf_op jit(solution)/shard_map/reduce_sum | solution.py:31
  222.2 15.5 %broadcast_multiply_fusion.1 = (f32[32,8,64,64]{3,2,1,0:T(8,128)}, f32[32,8,64]{2,1,0:T(8,128)S(1)}, f32[32,8,64,64]{3,2,1,0:T(8,128)}) fusion(f32[32,8,64]{2,1,0:T(8,128)} %get-tuple-element.31, f32[32,8,64]{2,1,0:T(8,128)} %neg.42, f32[32,8,64]{2,1,0:T(8,128)} %get-tuple-element.33, f32[32,8,64]{2,1,0:T(8,128)} %get-tuple-element.40, ...), kind=kLoop, calls=%fused_computation.19 | loop fusion | flops 13615104 | bytes 13369376 | tf_op jit(solution)/shard_map/mul | solution.py:28
  242.0 2.8 fusion.19
  246.2 4.5 %all-to-all-start.2 = ((bf16[8,4,512]{2,1,0:T(4,128)(2,1)}), bf16[8,4,512]{2,1,0:T(4,128)(2,1)S(1)}, u32[]{:S(2)}, u32[]{:S(2)}) async-start(bf16[8,4,512]{2,1,0:T(4,128)(2,1)} %reshape.356), calls=%async_computation.3 | async-start | bytes 65536 | tf_op jit(solution)/shard_map/all_to_all | solution.py:156
  250.9 4.6 %all-to-all-done.2 = bf16[8,4,512]{2,1,0:T(4,128)(2,1)S(1)} async-done(((bf16[8,4,512]{2,1,0:T(4,128)(2,1)}), bf16[8,4,512]{2,1,0:T(4,128)(2,1)S(1)}, u32[]{:S(2)}, u32[]{:S(2)}) %all-to-all-start.2) | async-done | bytes 32800 | tf_op jit(solution)/shard_map/all_to_all | solution.py:156
  256.3 14.6 %all_gather.27 = bf16[32,2048]{1,0:T(8,128)(2,1)S(1)} all-gather(bf16[32,512]{1,0:T(8,128)(2,1)S(1)} %gather_fusion.5), channel_id=1, replica_groups=mesh['req'=8,'mdl'=4] {'mdl'}, dimensions={1}, use_global_device_ids=true | all-gather | bytes 163840 | tf_op jit(solution)/shard_map/all_gather | solution.py:166
  271.2 3.7 mul.597
  274.9 8.1 %mul.647 = f32[32,8,4096]{2,1,0:T(8,128)} reshape(f32[32,8,64,64]{3,2,1,0:T(8,128)} %mul.597) | data formatting | bytes 8388608 | tf_op jit(solution)/shard_map/mul | solution.py:27
  283.0 3.7 mul.561
  286.7 7.9 %mul.639 = f32[32,8,4096]{2,1,0:T(8,128)} reshape(f32[32,8,64,64]{3,2,1,0:T(8,128)} %mul.561) | data formatting | bytes 8388608 | tf_op jit(solution)/shard_map/mul | solution.py:27
  294.6 3.7 mul.579
  298.3 7.9 %mul.643 = f32[32,8,4096]{2,1,0:T(8,128)} reshape(f32[32,8,64,64]{3,2,1,0:T(8,128)} %mul.579) | data formatting | bytes 8388608 | tf_op jit(solution)/shard_map/mul | solution.py:27
  306.2 3.7 mul.523
  309.9 7.9 %mul.635 = f32[32,8,4096]{2,1,0:T(8,128)} reshape(f32[32,8,64,64]{3,2,1,0:T(8,128)} %mul.523) | data formatting | bytes 8388608 | tf_op jit(solution)/shard_map/mul | solution.py:27
  317.8 7.9 %mul.637 = f32[32,8,4096]{2,1,0:T(8,128)} reshape(f32[32,8,64,64]{3,2,1,0:T(8,128)} %get-tuple-element.52) | data formatting | bytes 8388608 | tf_op jit(solution)/shard_map/mul | solution.py:28
  325.7 7.9 %mul.638 = f32[32,8,4096]{2,1,0:T(8,128)} reshape(f32[32,8,64,64]{3,2,1,0:T(8,128)} %get-tuple-element.53) | data formatting | bytes 8388608 | tf_op jit(solution)/shard_map/mul | solution.py:29
  333.6 7.9 %mul.641 = f32[32,8,4096]{2,1,0:T(8,128)} reshape(f32[32,8,64,64]{3,2,1,0:T(8,128)} %get-tuple-element.54) | data formatting | bytes 8388608 | tf_op jit(solution)/shard_map/mul | solution.py:28
  341.5 7.9 %mul.642 = f32[32,8,4096]{2,1,0:T(8,128)} reshape(f32[32,8,64,64]{3,2,1,0:T(8,128)} %get-tuple-element.55) | data formatting | bytes 8388608 | tf_op jit(solution)/shard_map/mul | solution.py:29
  349.4 7.9 %mul.645 = f32[32,8,4096]{2,1,0:T(8,128)} reshape(f32[32,8,64,64]{3,2,1,0:T(8,128)} %get-tuple-element.56) | data formatting | bytes 8388608 | tf_op jit(solution)/shard_map/mul | solution.py:28
  357.3 7.9 %mul.646 = f32[32,8,4096]{2,1,0:T(8,128)} reshape(f32[32,8,64,64]{3,2,1,0:T(8,128)} %get-tuple-element.57) | data formatting | bytes 8388608 | tf_op jit(solution)/shard_map/mul | solution.py:29
  365.2 7.9 %mul.649 = f32[32,8,4096]{2,1,0:T(8,128)} reshape(f32[32,8,64,64]{3,2,1,0:T(8,128)} %get-tuple-element.58) | data formatting | bytes 8388608 | tf_op jit(solution)/shard_map/mul | solution.py:28
  373.1 7.9 %mul.650 = f32[32,8,4096]{2,1,0:T(8,128)} reshape(f32[32,8,64,64]{3,2,1,0:T(8,128)} %get-tuple-element.60) | data formatting | bytes 8388608 | tf_op jit(solution)/shard_map/mul | solution.py:29
  382.2 16.0 %all_gather.26 = bf16[32,4,2048]{2,1,0:T(4,128)(2,1)S(1)} all-gather(bf16[32,4,512]{2,1,0:T(4,128)(2,1)S(1)} %add_convert_fusion.6), channel_id=1, replica_groups=mesh['req'=8,'mdl'=4] {'mdl'}, dimensions={2}, use_global_device_ids=true | all-gather | bytes 655360 | tf_op jit(solution)/shard_map/all_gather | solution.py:227
  400.7 5.6 %convolution_convert_fusion = bf16[128,2048]{1,0:T(8,128)(2,1)} fusion(bf16[1024,2048]{1,0:T(8,128)(2,1)} %param.41, bf16[128,2048]{1,0:T(8,128)(2,1)S(1)} %reshape.351, bf16[2048,1024]{1,0:T(8,128)(2,1)} %param.40), kind=kOutput, calls=%fused_computation.29 | convolution fusion | flops 1074397184 | bytes 9437184 | tf_op jit(solution)/shard_map/dot_general | solution.py:14
  406.3 22.3 %add_select_fusion = f32[32,8,4096]{2,1,0:T(8,128)} fusion(f32[32,8,4096]{2,1,0:T(8,128)} %mul.650, f32[32,8,4096]{2,1,0:T(8,128)} %mul.649, f32[32,8,4096]{2,1,0:T(8,128)} %mul.647, f32[32,8,4096]{2,1,0:T(8,128)} %mul.646, f32[32,8,4096]{2,1,0:T(8,128)} %mul.645, f32[32,8,4096]{2,1,0:T(8,128)} %mul.643, f32[32,8,4096]{2,1,0:T(8,128)} %mul.642, ...), kind=kLoop, calls=%fused_computation.17 | loop fusion | flops 16777216 | bytes 58720384 | tf_op jit(solution)/shard_map/jit(_where)/select_n | solution.py:32
  428.6 2.0 multiply_reduce_fusion.10
  (162 shorter events, 57.8 us)
Async XLA Ops:
  7.2 234.8 %copy-start = (bf16[512,2048]{1,0:T(8,128)(2,1)S(1)}, bf16[512,2048]{1,0:T(8,128)(2,1)}, u32[]{:S(2)}) copy-start(bf16[512,2048]{1,0:T(8,128)(2,1)} %param.33) | copy-start | bytes 6291460
  7.2 147.5 %all-gather.2.cloned.1.call-start = ((), (), s32[]{:S(2)}) async-start(), calls=%async_computation.5 | async-start | bytes 1310720 | tf_op jit(solution)/shard_map/all_gather | solution.py:185
  10.3 79.1 %copy-start.20 = (s32[1024]{0:T(1024)}, s32[1024]{0:T(1024)S(1)}, u32[]{:S(2)}) copy-start(s32[1024]{0:T(1024)S(1)} %pad_clamp_fusion.1) | copy-start | bytes 12292
  12.3 77.0 %all-to-all-start.1 = ((bf16[8,4,512]{2,1,0:T(4,128)(2,1)}), bf16[8,4,512]{2,1,0:T(4,128)(2,1)S(1)}, u32[]{:S(2)}, u32[]{:S(2)}) async-start(bf16[8,4,512]{2,1,0:T(4,128)(2,1)} %reshape.354), calls=%async_computation.1 | async-start | bytes 65536 | tf_op jit(solution)/shard_map/all_to_all | solution.py:155
  25.9 63.5 %copy-start.11 = (f32[1,2048]{1,0:T(1,128)}, f32[1,2048]{1,0:T(1,128)S(1)}, u32[]{:S(2)}) copy-start(f32[1,2048]{1,0:T(1,128)S(1)} %get-tuple-element.70) | copy-start | bytes 24580
  25.9 63.5 %copy-start.12 = (f32[1,2048]{1,0:T(1,128)}, f32[1,2048]{1,0:T(1,128)S(1)}, u32[]{:S(2)}) copy-start(f32[1,2048]{1,0:T(1,128)S(1)} %get-tuple-element.71) | copy-start | bytes 24580
  78.9 10.5 %copy-start.10 = (f32[32,4]{1,0:T(8,128)}, f32[32,4]{1,0:T(8,128)S(1)}, u32[]{:S(2)}) copy-start(f32[32,4]{1,0:T(8,128)S(1)} %add_sqrt_fusion.3) | copy-start | bytes 1540
  80.4 13.8 %copy-start.21 = (s32[1024]{0:T(1024)}, s32[1024]{0:T(1024)S(1)}, u32[]{:S(2)}) copy-start(s32[1024]{0:T(1024)S(1)} %pad_clamp_fusion) | copy-start | bytes 12292
  89.4 67.7 %all-to-all-start = ((f32[8,4,8,4096]{3,2,1,0:T(8,128)}), f32[8,4,8,4096]{3,2,1,0:T(8,128)}, u32[]{:S(2)}, u32[]{:S(2)}) async-start(f32[8,4,8,4096]{3,2,1,0:T(8,128)} %bitcast.175), calls=%async_computation | async-start | bytes 8388608 | tf_op jit(solution)/shard_map/all_to_all | solution.py:154
  94.2 286.9 %reduce-scatter.3.cloned.1.call-start = ((), (), s32[]{:S(2)}) async-start(), calls=%async_computation.6 | async-start | bytes 1310720 | tf_op jit(solution)/shard_map/reduce_scatter | solution.py:223
  162.2 14.1 %copy-start.5 = (f32[32,8,64]{2,1,0:T(8,128)S(1)}, f32[32,8,64]{2,1,0:T(8,128)}, u32[]{:S(2)}) copy-start(f32[32,8,64]{2,1,0:T(8,128)} %copy.91) | copy-start | bytes 196612
  162.2 14.1 %copy-start.19 = (pred[32]{0:T(512)(128)(4,1)S(1)}, pred[32]{0:T(512)(128)(4,1)}, u32[]{:S(2)}) copy-start(pred[32]{0:T(512)(128)(4,1)} %get-tuple-element.83) | copy-start | bytes 100
  170.5 5.8 %copy-start.2 = (f32[32,8,64,64]{3,2,1,0:T(8,128)S(1)}, f32[32,8,64,64]{3,2,1,0:T(8,128)}, u32[]{:S(2)}) copy-start(f32[32,8,64,64]{3,2,1,0:T(8,128)} %reshape.338) | copy-start | bytes 12582916
  170.5 5.8 %copy-start.8 = (f32[32,8,64]{2,1,0:T(8,128)S(1)}, f32[32,8,64]{2,1,0:T(8,128)}, u32[]{:S(2)}) copy-start(f32[32,8,64]{2,1,0:T(8,128)} %get-tuple-element.35) | copy-start | bytes 196612
  170.5 18.2 %copy-start.22 = (pred[32]{0:T(512)(128)(4,1)S(1)}, pred[32]{0:T(512)(128)(4,1)}, u32[]{:S(2)}) copy-start(pred[32]{0:T(512)(128)(4,1)} %get-tuple-element.82) | copy-start | bytes 100
  188.7 19.5 %copy-start.4 = (f32[32,8,64]{2,1,0:T(8,128)S(1)}, f32[32,8,64]{2,1,0:T(8,128)}, u32[]{:S(2)}) copy-start(f32[32,8,64]{2,1,0:T(8,128)} %copy.96) | copy-start | bytes 196612
  188.7 19.5 %copy-start.18 = (pred[32]{0:T(512)(128)(4,1)S(1)}, pred[32]{0:T(512)(128)(4,1)}, u32[]{:S(2)}) copy-start(pred[32]{0:T(512)(128)(4,1)} %get-tuple-element.81) | copy-start | bytes 100
  208.3 13.9 %copy-start.7 = (f32[32,8,64]{2,1,0:T(8,128)S(1)}, f32[32,8,64]{2,1,0:T(8,128)}, u32[]{:S(2)}) copy-start(f32[32,8,64]{2,1,0:T(8,128)} %get-tuple-element.49) | copy-start | bytes 196612
  222.2 19.8 %copy-start.16 = (f32[1,512]{1,0:T(1,128)S(1)}, f32[1,512]{1,0:T(1,128)}, u32[]{:S(2)}) copy-start(f32[1,512]{1,0:T(1,128)} %get-tuple-element.73) | copy-start | bytes 6148
  222.2 19.8 %copy-start.17 = (f32[1,512]{1,0:T(1,128)S(1)}, f32[1,512]{1,0:T(1,128)}, u32[]{:S(2)}) copy-start(f32[1,512]{1,0:T(1,128)} %get-tuple-element.79) | copy-start | bytes 6148
  237.7 7.1 %copy-start.3 = (bf16[32,512]{1,0:T(8,128)(2,1)S(1)}, bf16[32,512]{1,0:T(8,128)(2,1)}, u32[]{:S(2)}) copy-start(bf16[32,512]{1,0:T(8,128)(2,1)} %param.26) | copy-start | bytes 98308
  237.7 13.0 %copy-start.26 = (s32[32]{0:T(128)S(1)}, s32[32]{0:T(128)}, u32[]{:S(2)}) copy-start(s32[32]{0:T(128)} %param.22) | copy-start | bytes 388
  237.7 13.1 %copy-start.24 = (pred[32,4]{0,1:T(4,128)(4,1)S(1)}, pred[32,4]{0,1:T(4,128)(4,1)}, u32[]{:S(2)}) copy-start(pred[32,4]{0,1:T(4,128)(4,1)} %get-tuple-element.84) | copy-start | bytes 388
  246.2 9.4 %all-to-all-start.2 = ((bf16[8,4,512]{2,1,0:T(4,128)(2,1)}), bf16[8,4,512]{2,1,0:T(4,128)(2,1)S(1)}, u32[]{:S(2)}, u32[]{:S(2)}) async-start(bf16[8,4,512]{2,1,0:T(4,128)(2,1)} %reshape.356), calls=%async_computation.3 | async-start | bytes 65536 | tf_op jit(solution)/shard_map/all_to_all | solution.py:156
  250.7 179.8 %reduce-scatter.5.cloned.1.call-start = ((), (), s32[]{:S(2)}) async-start(), calls=%async_computation.7 | async-start | bytes 655360 | tf_op jit(solution)/shard_map/reduce_scatter | solution.py:239
  274.9 8.1 %copy-start.6 = (f32[32,8,64]{2,1,0:T(8,128)S(1)}, f32[32,8,64]{2,1,0:T(8,128)}, u32[]{:S(2)}) copy-start(f32[32,8,64]{2,1,0:T(8,128)} %get-tuple-element.50) | copy-start | bytes 196612
  373.1 9.0 %copy-start.9 = (bf16[32,4,512]{2,1,0:T(4,128)(2,1)S(1)}, bf16[32,4,512]{2,1,0:T(4,128)(2,1)}, u32[]{:S(2)}) copy-start(bf16[32,4,512]{2,1,0:T(4,128)(2,1)} %param.21) | copy-start | bytes 393220
  373.1 25.9 %copy-start.13 = (f32[1,2048]{1,0:T(1,128)S(1)}, f32[1,2048]{1,0:T(1,128)}, u32[]{:S(2)}) copy-start(f32[1,2048]{1,0:T(1,128)} %get-tuple-element.69) | copy-start | bytes 24580
  373.1 25.9 %copy-start.14 = (f32[1,2048]{1,0:T(1,128)S(1)}, f32[1,2048]{1,0:T(1,128)}, u32[]{:S(2)}) copy-start(f32[1,2048]{1,0:T(1,128)} %get-tuple-element.72) | copy-start | bytes 24580
  373.1 26.3 %copy-start.15 = (f32[1,2048]{1,0:T(1,128)S(1)}, f32[1,2048]{1,0:T(1,128)}, u32[]{:S(2)}) copy-start(f32[1,2048]{1,0:T(1,128)} %get-tuple-element.62) | copy-start | bytes 24580
  382.2 24.1 %copy-start.23 = (pred[32]{0:T(512)(128)(4,1)S(1)}, pred[32]{0:T(512)(128)(4,1)}, u32[]{:S(2)}) copy-start(pred[32]{0:T(512)(128)(4,1)} %get-tuple-element.82) | copy-start | bytes 100
  382.2 24.1 %copy-start.25 = (pred[32]{0:T(512)(128)(4,1)S(1)}, pred[32]{0:T(512)(128)(4,1)}, u32[]{:S(2)}) copy-start(pred[32]{0:T(512)(128)(4,1)} %get-tuple-element.80) | copy-start | bytes 100
  406.3 26.0 %copy-start.1 = (bf16[512,2048]{1,0:T(8,128)(2,1)S(1)}, bf16[512,2048]{1,0:T(8,128)(2,1)}, u32[]{:S(2)}) copy-start(bf16[512,2048]{1,0:T(8,128)(2,1)} %param.33) | copy-start | bytes 6291460
Sparse Core Ops, SparseCore 0:
  9.6 36.9 all-gather.1
  244.9 30.9 reduce-scatter.2
  406.4 20.1 reduce-scatter.4
where the time goes:
time: 445 us; the launch traced here: 439 us
  local copies, waits for them, and re-layouts  175 us (39%)
  other arithmetic  112 us (25%)
  blocking collectives  94.6 us (21%)
  matrix products  23 us (5%)
  starting transfers between devices  14.6 us (3%)
  between operations  14.5 us (3%)
  waiting for transfers between devices  5.32 us (1%)
    mul x9, local copies, waits for them, and re-layouts, advance(): wkv_square * decay_now[:, :, None, :]  48.5 us
    mul x10, local copies, waits for them, and re-layouts, advance(): value_now[..., None] * key_now[:, :, None, :]  37.6 us
    mul x4, local copies, waits for them, and re-layouts, advance(): removal[..., None] * (unit_now * alpha_now)[:, :, None, :]  31.6 us
    reduce_sum x2, other arithmetic, advance(): removal = -jnp.sum(wkv_square * unit_now[:, :, None, :], axis=-1)  24.5 us
    reduce_sum x2, other arithmetic, advance(): jnp.sum(updated * recept_now[:, :, None, :], axis=-1)  23.4 us
    dot_general x8, matrix products, project(): return jnp.dot(inputs, weight, preferred_element_type=jnp.float32)  23 us
    select_n x1, other arithmetic, advance(): jnp.where(is_valid[:, None, None, None], updated, wkv_square)  22.3 us
    all_gather x1, blocking collectives, per_device(): lax.all_gather(decay_down, 'mdl', axis=0, tiled=True)  20.2 us
  transfers between devices with their start and end apart: 6, of which 1 were waited for; matrix products, arithmetic and copies ran while one was open for 48% of the time, Pallas kernels for 0%

commit v1 on v0

--- a/solution.py
+++ b/solution.py
@@ -2,6 +2,28 @@
 import jax.numpy as jnp
 from jax import lax
 from jax.sharding import PartitionSpec as P
+
+
+def split_up(shard, dim, count):
+    before, after = (shard.shape[:dim], shard.shape[dim + 1 :])
+    return jnp.moveaxis(shard.reshape(*before, count, -1, *after), dim, 0)
+
+
+def laid_out(blocks, dim):
+    blocks = jnp.moveaxis(blocks, 0, dim)
+    lengths = blocks.shape
+    return blocks.reshape(*lengths[:dim], lengths[dim] * lengths[dim + 1], *lengths[dim + 2 :])
+
+
+def swapped_with_each(x, axis, split_dim, concat_dim):
+    devices, index = (lax.axis_size(axis), lax.axis_index(axis))
+    tiles = split_up(x, split_dim, devices)
+    finished = [tiles[index]]
+    for step in range(1, devices):
+        sent = tiles[index ^ step]
+        finished.append(lax.ppermute(sent, axis, [(i, i ^ step) for i in range(devices)]))
+    tiles = jnp.stack(finished)[index ^ jnp.arange(devices)]
+    return laid_out(tiles, concat_dim)
 
 
 def layer_norm(stream, gain_row, offset):
@@ -153,7 +175,7 @@
     got_state, got_att, got_ffn = (
         lax.all_to_all(sent_state, "req", split_axis=0, concat_axis=0, tiled=True),
         lax.all_to_all(sent_att, "req", split_axis=0, concat_axis=0, tiled=True),
-        lax.all_to_all(sent_ffn, "req", split_axis=0, concat_axis=0, tiled=True),
+        swapped_with_each(sent_ffn, "req", 0, 0),
     )
     moved_state = got_state.reshape((sequence_batch_count,) + wkv_state.shape[1:])[placing]
     moved_att = got_att.reshape(sequence_batch_count, local_width)[placing].astype(jnp.bfloat16)

time: 445 us -> 451 us (1.013)
  local copies, waits for them, and re-layouts: 175 us -> 180 us
    ppermute x0 -> x7, starting transfers between devices: none -> 7.73 us  [swapped_with_each(): lax.ppermute(sent, axis, [(i, i ^ step) for i in range(devices)])]
    all_to_all x1 -> x0, waiting for transfers between devices: 4.6 us -> none  [per_device(): lax.all_to_all(sent_ffn, 'req', split_axis=0, concat_axis=0, tiled=True)]
    all_to_all x1 -> x0, starting transfers between devices: 4.53 us -> none  [per_device(): lax.all_to_all(sent_ffn, 'req', split_axis=0, concat_axis=0, tiled=True)]
  transfers between devices with their start and end apart: 6 -> 12, of which waited for: 1 -> 2; matrix products, arithmetic and copies ran while one was open for 48% -> 69% of each run, Pallas kernels for 0% -> 0%
where the time goes in v1:
time: 451 us; the launch traced here: 445 us
  local copies, waits for them, and re-layouts  180 us (40%)
  other arithmetic  113 us (25%)
  blocking collectives  92.7 us (21%)
  matrix products  23 us (5%)
  starting transfers between devices  16.3 us (4%)
  between operations  14.6 us (3%)
  waiting for transfers between devices  4.84 us (1%)
    mul x9, local copies, waits for them, and re-layouts, advance(): wkv_square * decay_now[:, :, None, :]  48.5 us
    mul x10, local copies, waits for them, and re-layouts, advance(): value_now[..., None] * key_now[:, :, None, :]  37.6 us
    mul x4, local copies, waits for them, and re-layouts, advance(): removal[..., None] * (unit_now * alpha_now)[:, :, None, :]  31.6 us
    reduce_sum x2, other arithmetic, advance(): removal = -jnp.sum(wkv_square * unit_now[:, :, None, :], axis=-1)  24.5 us
    reduce_sum x2, other arithmetic, advance(): jnp.sum(updated * recept_now[:, :, None, :], axis=-1)  23.4 us
    dot_general x8, matrix products, project(): return jnp.dot(inputs, weight, preferred_element_type=jnp.float32)  23 us
    select_n x1, other arithmetic, advance(): jnp.where(is_valid[:, None, None, None], updated, wkv_square)  22.3 us
    all_gather x1, blocking collectives, per_device(): lax.all_gather(decay_down, 'mdl', axis=0, tiled=True)  17.5 us
  transfers between devices with their start and end apart: 12, of which 2 were waited for; matrix products, arithmetic and copies ran while one was open for 69% of the time, Pallas kernels for 0%

profile of v1, /device:TPU:0, one launch (start us, length us, event | category | flops | bytes accessed | tf_op | source)
XLA Modules:
  0.0 444.6 jit_solution(396285596970733807)
XLA Ops:
  12.4 3.3 collective-permute-start.6
  20.3 3.9 all-to-all-start.1
  35.6 17.5 %all_gather.23 = bf16[2048,96]{0,1:T(8,128)(2,1)} all-gather(bf16[512,96]{0,1:T(8,128)(2,1)} %param.34), channel_id=1, replica_groups=mesh['req'=8,'mdl'=4] {'mdl'}, dimensions={0}, use_global_device_ids=true | all-gather | bytes 491520 | tf_op jit(solution)/shard_map/all_gather | solution.py:205
  53.1 15.3 %all_gather.24 = bf16[2048,96]{0,1:T(8,128)(2,1)S(1)} all-gather(bf16[512,96]{0,1:T(8,128)(2,1)} %param.36), channel_id=1, replica_groups=mesh['req'=8,'mdl'=4] {'mdl'}, dimensions={0}, use_global_device_ids=true | all-gather | bytes 491520 | tf_op jit(solution)/shard_map/all_gather | solution.py:206
  68.5 15.5 %all_gather.21 = bf16[32,4,2048]{2,1,0:T(4,128)(2,1)S(1)} all-gather(bf16[32,4,512]{2,1,0:T(4,128)(2,1)} %param.21), channel_id=1, replica_groups=mesh['req'=8,'mdl'=4] {'mdl'}, dimensions={2}, use_global_device_ids=true | all-gather | bytes 655360 | tf_op jit(solution)/shard_map/all_gather | solution.py:183
  86.8 3.9 copy.89
  90.7 5.0 %gather_fusion = f32[32,8,4096]{2,1,0:T(8,128)} fusion(f32[32,8,4096]{2,1,0:T(8,128)} %param.24, s32[1024]{0:T(1024)S(1)} %pad_clamp_fusion.2), kind=kCustom, calls=%fused_computation | custom fusion | bytes 8388736 | tf_op jit(solution)/shard_map/gather | solution.py:172
  95.7 4.6 %all-to-all-start = ((f32[8,4,8,4096]{3,2,1,0:T(8,128)}), f32[8,4,8,4096]{3,2,1,0:T(8,128)}, u32[]{:S(2)}, u32[]{:S(2)}) async-start(f32[8,4,8,4096]{3,2,1,0:T(8,128)} %bitcast.206), calls=%async_computation | async-start | bytes 8388608 | tf_op jit(solution)/shard_map/all_to_all | solution.py:176
  101.0 13.9 %all_gather.22 = bf16[32,2048]{1,0:T(8,128)(2,1)S(1)} all-gather(bf16[32,512]{1,0:T(8,128)(2,1)S(1)} %gather_fusion.3), channel_id=1, replica_groups=mesh['req'=8,'mdl'=4] {'mdl'}, dimensions={1}, use_global_device_ids=true | all-gather | bytes 163840 | tf_op jit(solution)/shard_map/all_gather | solution.py:187
  115.2 3.5 add_convert_fusion.1
  118.7 2.0 reshape.365
  120.6 2.2 fusion.63
  124.6 1.9 reshape.369
  126.5 4.4 add_convert_fusion.5
  135.9 2.2 broadcast_add_fusion
  138.2 2.5 fusion.39
  143.3 3.8 broadcast_multiply_fusion.8
  161.1 2.3 fusion.23
  163.4 5.1 %gather_fusion.1 = f32[32,8,4096]{2,1,0:T(8,128)} fusion(f32[32,8,4096]{2,1,0:T(8,128)} %bitcast.1, s32[1024]{0:T(1024)} %copy-done.21), kind=kCustom, calls=%fused_computation.1 | custom fusion | bytes 8388736 | tf_op jit(solution)/shard_map/gather | solution.py:180
  168.6 8.0 %reshape.359 = f32[32,8,64,64]{3,2,1,0:T(8,128)} reshape(f32[32,8,4096]{2,1,0:T(8,128)} %gather_fusion.1) | data formatting | bytes 8388608 | tf_op jit(solution)/shard_map/reshape | solution.py:83
  176.6 5.8 %multiply_reduce_fusion.7 = f32[32,8,64]{2,1,0:T(8,128)S(1)} fusion(f32[32,8,64,64]{3,2,1,0:T(8,128)} %reshape.359, f32[32,8,64]{2,1,0:T(8,128)S(1)} %get-tuple-element.98), kind=kLoop, calls=%fused_computation.17 | loop fusion | flops 2080768 | bytes 4325376 | tf_op jit(solution)/shard_map/reduce_sum | solution.py:47
  182.4 11.0 %multiply_reduce_fusion.6 = (f32[32,8,64]{2,1,0:T(8,128)S(1)}, f32[32,8,64]{2,1,0:T(8,128)S(1)}) fusion(f32[32,8,64]{2,1,0:T(8,128)S(1)} %copy-done.7, f32[32,8,64,64]{3,2,1,0:T(8,128)S(1)} %copy-done.2, f32[32,8,64]{2,1,0:T(8,128)S(1)} %get-tuple-element.51, f32[32,8,64]{2,1,0:T(8,128)S(1)} %get-tuple-element.30, f32[32,8,64]{2,1,0:T(8,128)S(1)} %neg.38, ...), kind=kLoop, calls=%fused_computation.15 | loop fusion | flops 10452992 | bytes 4784160 | tf_op jit(solution)/shard_map/reduce_sum | solution.py:53
  194.8 18.7 %multiply_reduce_fusion.3 = (f32[32,8,64]{2,1,0:T(8,128)S(1)}, f32[32,8,64,64]{3,2,1,0:T(8,128)}, f32[32,8,64]{2,1,0:T(8,128)S(1)}, f32[32,8,64,64]{3,2,1,0:T(8,...) fusion(f32[32,8,64]{2,1,0:T(8,128)} %get-tuple-element.100, ...), kind=kLoop, calls=%fused_computation.11 | loop fusion | flops 16744448 | bytes 26083392 | tf_op jit(solution)/shard_map/reduce_sum | solution.py:47
  214.3 12.5 %multiply_reduce_fusion.2 = (f32[32,8,64]{2,1,0:T(8,128)S(1)}, f32[32,8,64]{2,1,0:T(8,128)S(1)}, f32[32,8,64,64]{3,2,1,0:T(8,128)}, f32[32,8,64,64]{3,2,1,0:T(8,128)}) fusion(f32[32,8,64]{2,1,0:T(8,128)} %get-tuple-element.34, f32[32,8,64,64]{3,2,1,0:T(8,128)} %get-tuple-element.18, f32[32,8,64]{2,1,0:T(8,128)S(1)} %get-tuple-element.48, ...), kind=kLoop, calls=%fused_computation.9 | loop fusion | flops 10452992 | bytes 13172768 | tf_op jit(solution)/shard_map/reduce_sum | solution.py:53
  228.2 15.5 %broadcast_multiply_fusion.1 = (f32[32,8,64,64]{3,2,1,0:T(8,128)}, f32[32,8,64]{2,1,0:T(8,128)S(1)}, f32[32,8,64,64]{3,2,1,0:T(8,128)}) fusion(f32[32,8,64]{2,1,0:T(8,128)} %get-tuple-element.31, f32[32,8,64]{2,1,0:T(8,128)} %neg.42, f32[32,8,64]{2,1,0:T(8,128)} %get-tuple-element.33, f32[32,8,64]{2,1,0:T(8,128)} %get-tuple-element.40, ...), kind=kLoop, calls=%fused_computation.20 | loop fusion | flops 13615104 | bytes 13369376 | tf_op jit(solution)/shard_map/mul | solution.py:50
  248.0 2.8 fusion.19
  254.7 3.0 collective-permute-done.2
  261.9 14.6 %all_gather.27 = bf16[32,2048]{1,0:T(8,128)(2,1)S(1)} all-gather(bf16[32,512]{1,0:T(8,128)(2,1)S(1)} %gather_fusion.6), channel_id=1, replica_groups=mesh['req'=8,'mdl'=4] {'mdl'}, dimensions={1}, use_global_device_ids=true | all-gather | bytes 163840 | tf_op jit(solution)/shard_map/all_gather | solution.py:188
  276.8 3.7 mul.597
  280.5 8.1 %mul.647 = f32[32,8,4096]{2,1,0:T(8,128)} reshape(f32[32,8,64,64]{3,2,1,0:T(8,128)} %mul.597) | data formatting | bytes 8388608 | tf_op jit(solution)/shard_map/mul | solution.py:49
  288.7 3.7 mul.561
  292.4 7.9 %mul.639 = f32[32,8,4096]{2,1,0:T(8,128)} reshape(f32[32,8,64,64]{3,2,1,0:T(8,128)} %mul.561) | data formatting | bytes 8388608 | tf_op jit(solution)/shard_map/mul | solution.py:49
  300.3 3.7 mul.579
  304.0 7.9 %mul.643 = f32[32,8,4096]{2,1,0:T(8,128)} reshape(f32[32,8,64,64]{3,2,1,0:T(8,128)} %mul.579) | data formatting | bytes 8388608 | tf_op jit(solution)/shard_map/mul | solution.py:49
  311.9 3.7 mul.523
  315.6 7.9 %mul.635 = f32[32,8,4096]{2,1,0:T(8,128)} reshape(f32[32,8,64,64]{3,2,1,0:T(8,128)} %mul.523) | data formatting | bytes 8388608 | tf_op jit(solution)/shard_map/mul | solution.py:49
  323.5 7.9 %mul.637 = f32[32,8,4096]{2,1,0:T(8,128)} reshape(f32[32,8,64,64]{3,2,1,0:T(8,128)} %get-tuple-element.52) | data formatting | bytes 8388608 | tf_op jit(solution)/shard_map/mul | solution.py:50
  331.4 7.9 %mul.638 = f32[32,8,4096]{2,1,0:T(8,128)} reshape(f32[32,8,64,64]{3,2,1,0:T(8,128)} %get-tuple-element.53) | data formatting | bytes 8388608 | tf_op jit(solution)/shard_map/mul | solution.py:51
  339.3 7.9 %mul.641 = f32[32,8,4096]{2,1,0:T(8,128)} reshape(f32[32,8,64,64]{3,2,1,0:T(8,128)} %get-tuple-element.54) | data formatting | bytes 8388608 | tf_op jit(solution)/shard_map/mul | solution.py:50
  347.2 7.9 %mul.642 = f32[32,8,4096]{2,1,0:T(8,128)} reshape(f32[32,8,64,64]{3,2,1,0:T(8,128)} %get-tuple-element.55) | data formatting | bytes 8388608 | tf_op jit(solution)/shard_map/mul | solution.py:51
  355.1 7.9 %mul.645 = f32[32,8,4096]{2,1,0:T(8,128)} reshape(f32[32,8,64,64]{3,2,1,0:T(8,128)} %get-tuple-element.56) | data formatting | bytes 8388608 | tf_op jit(solution)/shard_map/mul | solution.py:50
  363.0 7.9 %mul.646 = f32[32,8,4096]{2,1,0:T(8,128)} reshape(f32[32,8,64,64]{3,2,1,0:T(8,128)} %get-tuple-element.57) | data formatting | bytes 8388608 | tf_op jit(solution)/shard_map/mul | solution.py:51
  370.9 7.9 %mul.649 = f32[32,8,4096]{2,1,0:T(8,128)} reshape(f32[32,8,64,64]{3,2,1,0:T(8,128)} %get-tuple-element.58) | data formatting | bytes 8388608 | tf_op jit(solution)/shard_map/mul | solution.py:50
  378.8 7.9 %mul.650 = f32[32,8,4096]{2,1,0:T(8,128)} reshape(f32[32,8,64,64]{3,2,1,0:T(8,128)} %get-tuple-element.60) | data formatting | bytes 8388608 | tf_op jit(solution)/shard_map/mul | solution.py:51
  387.9 15.9 %all_gather.26 = bf16[32,4,2048]{2,1,0:T(4,128)(2,1)S(1)} all-gather(bf16[32,4,512]{2,1,0:T(4,128)(2,1)S(1)} %add_convert_fusion.6), channel_id=1, replica_groups=mesh['req'=8,'mdl'=4] {'mdl'}, dimensions={2}, use_global_device_ids=true | all-gather | bytes 655360 | tf_op jit(solution)/shard_map/all_gather | solution.py:249
  406.2 5.6 %convolution_convert_fusion = bf16[128,2048]{1,0:T(8,128)(2,1)} fusion(bf16[1024,2048]{1,0:T(8,128)(2,1)} %param.41, bf16[128,2048]{1,0:T(8,128)(2,1)S(1)} %reshape.371, bf16[2048,1024]{1,0:T(8,128)(2,1)} %param.40), kind=kOutput, calls=%fused_computation.30 | convolution fusion | flops 1074397184 | bytes 9437184 | tf_op jit(solution)/shard_map/dot_general | solution.py:36
  411.8 22.3 %add_select_fusion = f32[32,8,4096]{2,1,0:T(8,128)} fusion(f32[32,8,4096]{2,1,0:T(8,128)} %mul.650, f32[32,8,4096]{2,1,0:T(8,128)} %mul.649, f32[32,8,4096]{2,1,0:T(8,128)} %mul.647, f32[32,8,4096]{2,1,0:T(8,128)} %mul.646, f32[32,8,4096]{2,1,0:T(8,128)} %mul.645, f32[32,8,4096]{2,1,0:T(8,128)} %mul.643, f32[32,8,4096]{2,1,0:T(8,128)} %mul.642, ...), kind=kLoop, calls=%fused_computation.18 | loop fusion | flops 16777216 | bytes 58720384 | tf_op jit(solution)/shard_map/jit(_where)/select_n | solution.py:54
  434.1 2.0 multiply_reduce_fusion.10
  (189 shorter events, 69.7 us)
Async XLA Ops:
  7.2 240.9 %copy-start = (bf16[512,2048]{1,0:T(8,128)(2,1)S(1)}, bf16[512,2048]{1,0:T(8,128)(2,1)}, u32[]{:S(2)}) copy-start(bf16[512,2048]{1,0:T(8,128)(2,1)} %param.33) | copy-start | bytes 6291460
  7.2 153.9 %all-gather.2.cloned.1.call-start = ((), (), s32[]{:S(2)}) async-start(), calls=%async_computation.4 | async-start | bytes 1310720 | tf_op jit(solution)/shard_map/all_gather | solution.py:207
  12.4 247.4 %collective-permute-start.6 = (bf16[1,4,512]{2,1,0:T(4,128)(2,1)}, bf16[1,4,512]{2,1,0:T(4,128)(2,1)}, u32[]{:S(2)}, u32[]{:S(2)}) collective-permute-start(bf16[1,4,512]{2,1,0:T(4,128)(2,1)} %get-tuple-element.69), channel_id=1, source_target_pairs={{0,28},{4,24},{8,20},{12,16},{16,12},{20,8},{24,4},{28,0},{1,29},{... | collective-permute-start | bytes 12296 | tf_op jit(solution)/shard_map/ppermute | solution.py:24
  15.8 243.4 %collective-permute-start.5 = (bf16[1,4,512]{2,1,0:T(4,128)(2,1)}, bf16[1,4,512]{2,1,0:T(4,128)(2,1)}, u32[]{:S(2)}, u32[]{:S(2)}) collective-permute-start(bf16[1,4,512]{2,1,0:T(4,128)(2,1)} %get-tuple-element.70), channel_id=1, source_target_pairs={{0,24},{4,28},{8,16},{12,20},{16,8},{20,12},{24,0},{28,4},{1,25},{... | collective-permute-start | bytes 12296 | tf_op jit(solution)/shard_map/ppermute | solution.py:24
  16.4 242.0 %collective-permute-start.4 = (bf16[1,4,512]{2,1,0:T(4,128)(2,1)}, bf16[1,4,512]{2,1,0:T(4,128)(2,1)}, u32[]{:S(2)}, u32[]{:S(2)}) collective-permute-start(bf16[1,4,512]{2,1,0:T(4,128)(2,1)} %get-tuple-element.71), channel_id=1, source_target_pairs={{0,20},{4,16},{8,28},{12,24},{16,4},{20,0},{24,12},{28,8},{1,21},{... | collective-permute-start | bytes 12296 | tf_op jit(solution)/shard_map/ppermute | solution.py:24
  17.8 239.9 %collective-permute-start.3 = (bf16[1,4,512]{2,1,0:T(4,128)(2,1)}, bf16[1,4,512]{2,1,0:T(4,128)(2,1)}, u32[]{:S(2)}, u32[]{:S(2)}) collective-permute-start(bf16[1,4,512]{2,1,0:T(4,128)(2,1)} %get-tuple-element.72), channel_id=1, source_target_pairs={{0,16},{4,20},{8,24},{12,28},{16,0},{20,4},{24,8},{28,12},{1,17},{... | collective-permute-start | bytes 12296 | tf_op jit(solution)/shard_map/ppermute | solution.py:24
  18.1 232.9 %collective-permute-start = (bf16[1,4,512]{2,1,0:T(4,128)(2,1)}, bf16[1,4,512]{2,1,0:T(4,128)(2,1)}, u32[]{:S(2)}, u32[]{:S(2)}) collective-permute-start(bf16[1,4,512]{2,1,0:T(4,128)(2,1)} %get-tuple-element.75), channel_id=1, source_target_pairs={{0,4},{4,0},{8,12},{12,8},{16,20},{20,16},{24,28},{28,24},{1,5},{5... | collective-permute-start | bytes 12296 | tf_op jit(solution)/shard_map/ppermute | solution.py:24
  20.3 75.4 %all-to-all-start.1 = ((bf16[8,4,512]{2,1,0:T(4,128)(2,1)}), bf16[8,4,512]{2,1,0:T(4,128)(2,1)S(1)}, u32[]{:S(2)}, u32[]{:S(2)}) async-start(bf16[8,4,512]{2,1,0:T(4,128)(2,1)} %reshape.374), calls=%async_computation.1 | async-start | bytes 65536 | tf_op jit(solution)/shard_map/all_to_all | solution.py:177
  32.3 68.1 %copy-start.21 = (s32[1024]{0:T(1024)}, s32[1024]{0:T(1024)S(1)}, u32[]{:S(2)}) copy-start(s32[1024]{0:T(1024)S(1)} %pad_clamp_fusion.1) | copy-start | bytes 12292
  33.8 61.9 %copy-start.10 = (f32[1,2048]{1,0:T(1,128)}, f32[1,2048]{1,0:T(1,128)S(1)}, u32[]{:S(2)}) copy-start(f32[1,2048]{1,0:T(1,128)S(1)} %get-tuple-element.78) | copy-start | bytes 24580
  33.8 61.9 %copy-start.11 = (f32[1,2048]{1,0:T(1,128)}, f32[1,2048]{1,0:T(1,128)S(1)}, u32[]{:S(2)}) copy-start(f32[1,2048]{1,0:T(1,128)S(1)} %get-tuple-element.79) | copy-start | bytes 24580
  84.8 11.0 %copy-start.9 = (f32[32,4]{1,0:T(8,128)}, f32[32,4]{1,0:T(8,128)S(1)}, u32[]{:S(2)}) copy-start(f32[32,4]{1,0:T(8,128)S(1)} %add_sqrt_fusion.3) | copy-start | bytes 1540
  95.7 67.7 %all-to-all-start = ((f32[8,4,8,4096]{3,2,1,0:T(8,128)}), f32[8,4,8,4096]{3,2,1,0:T(8,128)}, u32[]{:S(2)}, u32[]{:S(2)}) async-start(f32[8,4,8,4096]{3,2,1,0:T(8,128)} %bitcast.206), calls=%async_computation | async-start | bytes 8388608 | tf_op jit(solution)/shard_map/all_to_all | solution.py:176
  100.3 286.4 %reduce-scatter.3.cloned.1.call-start = ((), (), s32[]{:S(2)}) async-start(), calls=%async_computation.5 | async-start | bytes 1310720 | tf_op jit(solution)/shard_map/reduce_scatter | solution.py:245
  168.6 13.8 %copy-start.4 = (f32[32,8,64]{2,1,0:T(8,128)S(1)}, f32[32,8,64]{2,1,0:T(8,128)}, u32[]{:S(2)}) copy-start(f32[32,8,64]{2,1,0:T(8,128)} %copy.91) | copy-start | bytes 196612
  168.6 13.8 %copy-start.20 = (pred[32]{0:T(512)(128)(4,1)S(1)}, pred[32]{0:T(512)(128)(4,1)}, u32[]{:S(2)}) copy-start(pred[32]{0:T(512)(128)(4,1)} %get-tuple-element.91) | copy-start | bytes 100
  176.5 5.8 %copy-start.2 = (f32[32,8,64,64]{3,2,1,0:T(8,128)S(1)}, f32[32,8,64,64]{3,2,1,0:T(8,128)}, u32[]{:S(2)}) copy-start(f32[32,8,64,64]{3,2,1,0:T(8,128)} %reshape.359) | copy-start | bytes 12582916
  176.6 5.8 %copy-start.7 = (f32[32,8,64]{2,1,0:T(8,128)S(1)}, f32[32,8,64]{2,1,0:T(8,128)}, u32[]{:S(2)}) copy-start(f32[32,8,64]{2,1,0:T(8,128)} %get-tuple-element.35) | copy-start | bytes 196612
  176.6 18.2 %copy-start.22 = (pred[32]{0:T(512)(128)(4,1)S(1)}, pred[32]{0:T(512)(128)(4,1)}, u32[]{:S(2)}) copy-start(pred[32]{0:T(512)(128)(4,1)} %get-tuple-element.90) | copy-start | bytes 100
  194.8 19.5 %copy-start.3 = (f32[32,8,64]{2,1,0:T(8,128)S(1)}, f32[32,8,64]{2,1,0:T(8,128)}, u32[]{:S(2)}) copy-start(f32[32,8,64]{2,1,0:T(8,128)} %copy.96) | copy-start | bytes 196612
  194.8 19.5 %copy-start.19 = (pred[32]{0:T(512)(128)(4,1)S(1)}, pred[32]{0:T(512)(128)(4,1)}, u32[]{:S(2)}) copy-start(pred[32]{0:T(512)(128)(4,1)} %get-tuple-element.89) | copy-start | bytes 100
  214.3 13.9 %copy-start.6 = (f32[32,8,64]{2,1,0:T(8,128)S(1)}, f32[32,8,64]{2,1,0:T(8,128)}, u32[]{:S(2)}) copy-start(f32[32,8,64]{2,1,0:T(8,128)} %get-tuple-element.49) | copy-start | bytes 196612
  228.2 19.9 %copy-start.17 = (f32[1,512]{1,0:T(1,128)S(1)}, f32[1,512]{1,0:T(1,128)}, u32[]{:S(2)}) copy-start(f32[1,512]{1,0:T(1,128)} %get-tuple-element.81) | copy-start | bytes 6148
  228.2 19.9 %copy-start.18 = (f32[1,512]{1,0:T(1,128)S(1)}, f32[1,512]{1,0:T(1,128)}, u32[]{:S(2)}) copy-start(f32[1,512]{1,0:T(1,128)} %get-tuple-element.87) | copy-start | bytes 6148
  243.7 7.2 %copy-start.28 = (s32[8]{0:T(128)S(1)}, s32[8]{0:T(128)}, u32[]{:S(2)}) copy-start(s32[8]{0:T(128)} %fusion.57) | copy-start | bytes 100
  243.7 7.2 %copy-start.26 = (pred[32,4]{0,1:T(4,128)(4,1)S(1)}, pred[32,4]{0,1:T(4,128)(4,1)}, u32[]{:S(2)}) copy-start(pred[32,4]{0,1:T(4,128)(4,1)} %get-tuple-element.92) | copy-start | bytes 388
  243.7 7.3 %copy-start.25 = (bf16[1,4,512]{2,1,0:T(4,128)(2,1)S(1)}, bf16[1,4,512]{2,1,0:T(4,128)(2,1)}, u32[]{:S(2)}) copy-start(bf16[1,4,512]{2,1,0:T(4,128)(2,1)} %get-tuple-element.74) | copy-start | bytes 12292
  243.7 9.2 %copy-start.15 = (bf16[8,1,4,512]{3,2,0,1:T(4,128)(2,1)S(1)}, bf16[8,1,4,512]{3,2,0,1:T(4,128)(2,1)}, u32[]{:S(2)}) copy-start(bf16[8,1,4,512]{3,2,0,1:T(4,128)(2,1)} %get-tuple-element.76) | copy-start | bytes 98308
  243.8 10.9 %copy-start.24 = (bf16[1,4,512]{2,1,0:T(4,128)(2,1)S(1)}, bf16[1,4,512]{2,1,0:T(4,128)(2,1)}, u32[]{:S(2)}) copy-start(bf16[1,4,512]{2,1,0:T(4,128)(2,1)} %get-tuple-element.73) | copy-start | bytes 12292
  250.8 185.3 %reduce-scatter.5.cloned.1.call-start = ((), (), s32[]{:S(2)}) async-start(), calls=%async_computation.6 | async-start | bytes 655360 | tf_op jit(solution)/shard_map/reduce_scatter | solution.py:261
  251.0 3.7 collective-permute-start.1
  254.7 3.0 collective-permute-start.2
  280.5 8.1 %copy-start.5 = (f32[32,8,64]{2,1,0:T(8,128)S(1)}, f32[32,8,64]{2,1,0:T(8,128)}, u32[]{:S(2)}) copy-start(f32[32,8,64]{2,1,0:T(8,128)} %get-tuple-element.50) | copy-start | bytes 196612
  378.8 9.0 %copy-start.8 = (bf16[32,4,512]{2,1,0:T(4,128)(2,1)S(1)}, bf16[32,4,512]{2,1,0:T(4,128)(2,1)}, u32[]{:S(2)}) copy-start(bf16[32,4,512]{2,1,0:T(4,128)(2,1)} %param.21) | copy-start | bytes 393220
  378.8 25.7 %copy-start.12 = (f32[1,2048]{1,0:T(1,128)S(1)}, f32[1,2048]{1,0:T(1,128)}, u32[]{:S(2)}) copy-start(f32[1,2048]{1,0:T(1,128)} %get-tuple-element.77) | copy-start | bytes 24580
  378.8 25.7 %copy-start.13 = (f32[1,2048]{1,0:T(1,128)S(1)}, f32[1,2048]{1,0:T(1,128)}, u32[]{:S(2)}) copy-start(f32[1,2048]{1,0:T(1,128)} %get-tuple-element.80) | copy-start | bytes 24580
  378.8 26.2 %copy-start.16 = (f32[1,2048]{1,0:T(1,128)S(1)}, f32[1,2048]{1,0:T(1,128)}, u32[]{:S(2)}) copy-start(f32[1,2048]{1,0:T(1,128)} %get-tuple-element.62) | copy-start | bytes 24580
  387.8 23.9 %copy-start.23 = (pred[32]{0:T(512)(128)(4,1)S(1)}, pred[32]{0:T(512)(128)(4,1)}, u32[]{:S(2)}) copy-start(pred[32]{0:T(512)(128)(4,1)} %get-tuple-element.90) | copy-start | bytes 100
  387.9 23.9 %copy-start.27 = (pred[32]{0:T(512)(128)(4,1)S(1)}, pred[32]{0:T(512)(128)(4,1)}, u32[]{:S(2)}) copy-start(pred[32]{0:T(512)(128)(4,1)} %get-tuple-element.88) | copy-start | bytes 100
  411.8 22.3 %copy-start.14 = (f32[32,4]{1,0:T(8,128)S(1)}, f32[32,4]{1,0:T(8,128)}, u32[]{:S(2)}) copy-start(f32[32,4]{1,0:T(8,128)} %fusion.54) | copy-start | bytes 1540
  411.8 26.0 %copy-start.1 = (bf16[512,2048]{1,0:T(8,128)(2,1)S(1)}, bf16[512,2048]{1,0:T(8,128)(2,1)}, u32[]{:S(2)}) copy-start(bf16[512,2048]{1,0:T(8,128)(2,1)} %param.33) | copy-start | bytes 6291460
Sparse Core Ops, SparseCore 0:
  9.6 30.6 all-gather.1
  250.9 30.2 reduce-scatter.2
  411.9 22.5 reduce-scatter.4
